TPU v7x, 512 devices: a whole 4x4x16 slice. The times are simulated.
512 devices in a mesh: grp: 16 (over y, z_hi, core), sub: 32 (over x, z_lo).
Axes of the slice: x: 4, y: 4, z: 16 (z_hi: 2, z_lo: 8; z = z_hi * 8 + z_lo), core: 2. Of those that a mesh axis runs over, the one named last changes fastest.
Arguments:
- activations: bfloat16 [262144, 2048], P(('grp', 'sub')), may hold values from -110 to 110
- norm_gain: float32 [2048], replicated, may hold values from 0.5 to 1.5
- key_weight: bfloat16 [2048, 768], P('sub'), may hold values from -0.125 to 0.125
- key_grads: bfloat16 [262144, 768], P(('grp', 'sub')), may hold values from -3 to 3
Outputs:
- input_grads: bfloat16 [262144, 2048], P(('grp', 'sub'))
- weight_grads: float32 [2048, 768], P('sub', 'grp')
- gain_grads: float32 [2048], P('sub')
All inputs are finite; a program needn't handle non-finite values.
Results may differ from a plain program's by a relative error of at most 0.0029.
Values may be sent and summed in bfloat16 or wider, within the bound.
A program may use at most 64 MiB of HBM per device.

v0:
```python
import jax
import jax.numpy as jnp
from jax import lax
from jax.sharding import PartitionSpec as P


def local(activations, norm_gain, key_weight, key_grads):
    inputs = activations.astype(jnp.float32)
    mean_square = jnp.mean(inputs * inputs, axis=1, keepdims=True)
    inverse_rms = lax.rsqrt(mean_square + 1e-05)
    normed = inputs * inverse_rms
    scaled = (normed * norm_gain).astype(jnp.bfloat16)
    grad_scaled = lax.dot_general(
        key_grads,
        lax.all_gather(key_weight, "sub", axis=0, tiled=True),
        (((1,), (1,)), ((), ())),
        preferred_element_type=jnp.float32,
    )
    gained = norm_gain * grad_scaled
    input_grads = (
        inverse_rms * (gained - normed * jnp.mean(gained * normed, axis=1, keepdims=True))
    ).astype(jnp.bfloat16)
    groups = lax.axis_size("grp")
    members = lax.axis_size("sub")
    feature_rows = key_weight.shape[0]
    key_width = key_grads.shape[1]
    term = lax.dot_general(
        scaled, key_grads, (((0,), (0,)), ((), ())), preferred_element_type=jnp.float32
    )
    received = lax.all_to_all(term, "sub", split_axis=0, concat_axis=1, tiled=True)
    shared = jnp.sum(received.reshape(feature_rows, members, key_width), axis=1)
    owned = lax.psum_scatter(shared, "grp", scatter_dimension=1, tiled=True)
    weight_grads = owned / groups
    local_gain = jnp.sum(grad_scaled * normed, axis=0)
    summed = lax.psum(local_gain, ("grp", "sub"))
    gain_sum = lax.dynamic_slice_in_dim(summed, lax.axis_index("sub") * feature_rows, feature_rows)
    gain_grads = gain_sum / groups
    return (input_grads, weight_grads, gain_grads)


def solution(mesh):
    return jax.shard_map(
        local,
        mesh=mesh,
        in_specs=(P(("grp", "sub"), None), P(), P("sub", None), P(("grp", "sub"), None)),
        out_specs=(P(("grp", "sub"), None), P("sub", "grp"), P("sub")),
        check_vma=False,
    )
```

profile of v0, /device:TPU:2, one launch (start us, length us, event | category | flops | bytes accessed | tf_op | source)
XLA Modules:
  0.0 569.9 jit_solution(18334966130599238533)
XLA Ops:
  8.0 0.0 copy-start
  8.0 2.1 fusion.10
  10.2 0.0 copy-done
  10.2 6.2 %fusion.11 = f32[2048,768]{1,0:T(8,128)} fusion(bf16[512,768]{1,0:T(8,128)(2,1)S(1)} %copy-done, bf16[512,2048]{1,0:T(8,128)(2,1)} %param.4, f32[2048]{0:T(1024)} %param.5, f32[512]{0:T(512)S(1)} %add_rsqrt_fusion), kind=kOutput, calls=%fused_computation.13 | convolution fusion | flops 1614807040 | bytes 9185280 | tf_op jit(solution)/shard_map/dot_general | solution.py:27
  16.4 0.0 copy-start.1
  16.4 0.0 copy-start.2
  16.4 15.9 %all-to-all-start = ((f32[32,64,768]{2,1,0:T(8,128)}), f32[32,64,768]{2,1,0:T(8,128)}, u32[]{:S(2)}, u32[]{:S(2)}) async-start(f32[32,64,768]{2,1,0:T(8,128)} %bitcast.6), calls=%async_computation | async-start | bytes 12582912 | tf_op jit(solution)/shard_map/all_to_all | solution.py:30
  32.2 0.0 all-gather.2.cloned.1.call-start
  32.3 0.7 all-gather.2.cloned.1.call-update
  33.0 0.0 reduce-scatter.4.cloned.1.call-start
  33.0 394.7 %all-gather.2.cloned.1.call-done = bf16[2048,768]{1,0:T(8,128)(2,1)} async-done(((bf16[64,768]{1,0:T(8,128)(2,1)}), bf16[2048,768]{1,0:T(8,128)(2,1)}) %all-gather.2.cloned.1.call-update) | async-done | bytes 3145744 | tf_op jit(solution)/shard_map/all_gather | solution.py:15
  427.7 0.0 copy-done.1
  427.7 0.0 copy-done.2
  427.7 6.0 %fusion.9 = (f32[2048]{0:T(1024)S(1)}, f32[512]{0:T(512)S(1)}, f32[512,2048]{1,0:T(8,128)}) fusion(bf16[512,2048]{1,0:T(8,128)(2,1)S(1)} %copy-done.1, f32[512]{0:T(512)S(1)} %add_rsqrt_fusion, f32[2048]{0:T(1024)S(1)} %copy-done.2, bf16[512,768]{1,0:T(8,128)(2,1)S(1)} %copy-done, bf16[2048,768]{1,0:T(8,128)(2,1)} %all-gather.2.cloned.1.call-done), kind=kOutput, calls=%fused_computation.11 | convolution fusion | flops 1617950208 | bytes 10244096 | tf_op jit(solution)/shard_map/dot_general | solution.py:13
  433.7 0.0 all-to-all-done
  433.7 3.1 reduce_sum.38
  436.8 0.9 copy.9
  437.7 0.0 reduce-scatter.4.cloned.1.call-update
  437.7 4.6 fusion.7
  442.3 118.0 %psum.7 = f32[2048]{0:T(1024)S(1)} all-reduce(f32[2048]{0:T(1024)S(1)} %get-tuple-element.9), channel_id=1, replica_groups=mesh['grp'=16,'sub'=32] {'grp','sub'}, use_global_device_ids=true, to_apply=%region_5.0 | all-reduce | flops 2048 | bytes 16384 | tf_op jit(solution)/shard_map/psum | solution.py:35
  560.3 0.6 dynamic-slice_multiply_fusion
  560.9 0.0 reduce-scatter.4.cloned.1.call-done
  560.9 0.8 copy.10
  561.7 0.7 copy.8
  (3 shorter events, 0.0 us)
Async XLA Ops:
  8.0 2.2 copy-start
  16.4 411.4 %copy-start.1 = (bf16[512,2048]{1,0:T(8,128)(2,1)S(1)}, bf16[512,2048]{1,0:T(8,128)(2,1)}, u32[]{:S(2)}) copy-start(bf16[512,2048]{1,0:T(8,128)(2,1)} %param.4) | copy-start | bytes 6291460
  16.4 411.4 %copy-start.2 = (f32[2048]{0:T(1024)S(1)}, f32[2048]{0:T(1024)}, u32[]{:S(2)}) copy-start(f32[2048]{0:T(1024)} %param.5) | copy-start | bytes 24580
  16.4 417.3 %all-to-all-start = ((f32[32,64,768]{2,1,0:T(8,128)}), f32[32,64,768]{2,1,0:T(8,128)}, u32[]{:S(2)}, u32[]{:S(2)}) async-start(f32[32,64,768]{2,1,0:T(8,128)} %bitcast.6), calls=%async_computation | async-start | bytes 12582912 | tf_op jit(solution)/shard_map/all_to_all | solution.py:30
  32.2 395.5 %all-gather.2.cloned.1.call-start = ((), (), s32[]{:S(2)}) async-start(), calls=%async_computation.2 | async-start | bytes 3244032 | tf_op jit(solution)/shard_map/all_gather | solution.py:15
  33.0 527.9 %reduce-scatter.4.cloned.1.call-start = ((), (), s32[]{:S(2)}) async-start(), calls=%async_computation.3 | async-start | bytes 417792
Sparse Core Ops, SparseCore 0:
  35.1 392.5 all-gather.1
Sparse Core Ops, SparseCore 1:
  437.8 106.9 reduce-scatter.3
where the time goes:
time: 570 us
  waiting for transfers between devices  395 us (69%)
  blocking collectives  118 us (21%)
  starting transfers between devices  15.9 us (3%)
  between operations  15.5 us (3%)
  matrix products  12.1 us (2%)
  other arithmetic  10.4 us (2%)
    all_gather x1, waiting for transfers between devices, local(): lax.all_gather(key_weight, 'sub', axis=0, tiled=True)  395 us
    psum x1, blocking collectives, local(): summed = lax.psum(local_gain, ('grp', 'sub'))  118 us
    all_to_all x1, starting transfers between devices, local(): lax.all_to_all(term, 'sub', split_axis=0, concat_axis=1, tiled=True)  15.9 us
  transfers between devices with their start and end apart: 3, of which 1 were waited for; matrix products, arithmetic and copies ran while one was open for 2% of the time, Pallas kernels for 0%

commit v1 on v0

--- a/solution.py
+++ b/solution.py
@@ -32,7 +32,9 @@
     owned = lax.psum_scatter(shared, "grp", scatter_dimension=1, tiled=True)
     weight_grads = owned / groups
     local_gain = jnp.sum(grad_scaled * normed, axis=0)
-    summed = lax.psum(local_gain, ("grp", "sub"))
+    summed = local_gain
+    for name in ("sub", "grp"):
+        summed = lax.psum(summed, name)
     gain_sum = lax.dynamic_slice_in_dim(summed, lax.axis_index("sub") * feature_rows, feature_rows)
     gain_grads = gain_sum / groups
     return (input_grads, weight_grads, gain_grads)

time: 570 us -> 648 us (1.14)
  the two profiles are of different devices: /device:TPU:2 before, /device:TPU:1 now
where the time goes in v1:
time: 648 us; the launch traced here: 647 us
  waiting for transfers between devices  393 us (61%)
  blocking collectives  198 us (31%)
  starting transfers between devices  16.2 us (2%)
  between operations  15.5 us (2%)
  matrix products  12.1 us (2%)
  other arithmetic  10.5 us (2%)
    all_gather x1, waiting for transfers between devices, local(): lax.all_gather(key_weight, 'sub', axis=0, tiled=True)  392 us
    psum x2, blocking collectives, local(): summed = lax.psum(summed, name)  198 us
    all_to_all x1, starting transfers between devices, local(): lax.all_to_all(term, 'sub', split_axis=0, concat_axis=1, tiled=True)  16.2 us
  transfers between devices with their start and end apart: 3, of which 1 were waited for; matrix products, arithmetic and copies ran while one was open for 2% of the time, Pallas kernels for 0%

profile of v1, /device:TPU:1, one launch (start us, length us, event | category | flops | bytes accessed | tf_op | source)
XLA Modules:
  0.0 647.4 jit_solution(6220572140583982227)
XLA Ops:
  8.0 0.0 copy-start
  8.0 2.1 fusion.10
  10.2 0.0 copy-done
  10.2 6.2 fusion.11
  16.4 0.0 copy-start.1
  16.4 0.0 copy-start.2
  16.4 16.2 %all-to-all-start = ((f32[32,64,768]{2,1,0:T(8,128)}), f32[32,64,768]{2,1,0:T(8,128)}, u32[]{:S(2)}, u32[]{:S(2)}) async-start(f32[32,64,768]{2,1,0:T(8,128)} %bitcast.6), calls=%async_computation | async-start | bytes 12582912 | tf_op jit(solution)/shard_map/all_to_all | solution.py:30
  32.5 0.0 all-gather.2.cloned.1.call-start
  32.6 0.7 all-gather.2.cloned.1.call-update
  33.3 0.0 reduce-scatter.4.cloned.1.call-start
  33.3 391.8 %all-gather.2.cloned.1.call-done = bf16[2048,768]{1,0:T(8,128)(2,1)} async-done(((bf16[64,768]{1,0:T(8,128)(2,1)}), bf16[2048,768]{1,0:T(8,128)(2,1)}) %all-gather.2.cloned.1.call-update) | async-done | bytes 3145744 | tf_op jit(solution)/shard_map/all_gather | solution.py:15
  425.2 0.0 copy-done.1
  425.2 0.0 copy-done.2
  425.2 6.0 fusion.9
  431.1 0.0 all-to-all-done
  431.1 3.1 reduce_sum.38
  434.2 0.9 copy.9
  435.1 0.0 reduce-scatter.4.cloned.1.call-update
  435.2 4.6 fusion.7
  439.7 106.7 %psum.14 = f32[2048]{0:T(1024)S(1)} all-reduce(f32[2048]{0:T(1024)S(1)} %get-tuple-element.9), channel_id=1, replica_groups=mesh['grp'=16,'sub'=32] {'sub'}, use_global_device_ids=true, to_apply=%region_5.0 | all-reduce | flops 2048 | bytes 16384 | tf_op jit(solution)/shard_map/psum | solution.py:37
  546.4 91.4 %psum.15 = f32[2048]{0:T(1024)S(1)} all-reduce(f32[2048]{0:T(1024)S(1)} %psum.14), channel_id=1, replica_groups=mesh['grp'=16,'sub'=32] {'grp'}, use_global_device_ids=true, to_apply=%region_6.0 | all-reduce | flops 2048 | bytes 16384 | tf_op jit(solution)/shard_map/psum | solution.py:37
  637.8 0.6 dynamic-slice_multiply_fusion
  638.4 0.0 reduce-scatter.4.cloned.1.call-done
  638.4 0.8 copy.10
  639.2 0.7 copy.8
  (3 shorter events, 0.0 us)
Async XLA Ops:
  8.0 2.2 copy-start
  16.4 408.8 %copy-start.1 = (bf16[512,2048]{1,0:T(8,128)(2,1)S(1)}, bf16[512,2048]{1,0:T(8,128)(2,1)}, u32[]{:S(2)}) copy-start(bf16[512,2048]{1,0:T(8,128)(2,1)} %param.4) | copy-start | bytes 6291460
  16.4 408.8 %copy-start.2 = (f32[2048]{0:T(1024)S(1)}, f32[2048]{0:T(1024)}, u32[]{:S(2)}) copy-start(f32[2048]{0:T(1024)} %param.5) | copy-start | bytes 24580
  16.4 414.7 %all-to-all-start = ((f32[32,64,768]{2,1,0:T(8,128)}), f32[32,64,768]{2,1,0:T(8,128)}, u32[]{:S(2)}, u32[]{:S(2)}) async-start(f32[32,64,768]{2,1,0:T(8,128)} %bitcast.6), calls=%async_computation | async-start | bytes 12582912 | tf_op jit(solution)/shard_map/all_to_all | solution.py:30
  32.5 392.6 %all-gather.2.cloned.1.call-start = ((), (), s32[]{:S(2)}) async-start(), calls=%async_computation.2 | async-start | bytes 3244032 | tf_op jit(solution)/shard_map/all_gather | solution.py:15
  33.3 605.1 %reduce-scatter.4.cloned.1.call-start = ((), (), s32[]{:S(2)}) async-start(), calls=%async_computation.3 | async-start | bytes 417792
Sparse Core Ops, SparseCore 0:
  35.4 389.6 all-gather.1
Sparse Core Ops, SparseCore 1:
  435.2 108.9 reduce-scatter.3
